TPU v7x, 32 devices: a whole 2x2x4 slice. The times are simulated.
32 devices in a mesh: dp: 4 (over y, core), fsdp: 8 (over z, x).
Axes of the slice: x: 2, y: 2, z: 4, core: 2. Of those that a mesh axis runs over, the one named last changes fastest.
Arguments:
- hidden_in: bfloat16 [2, 32, 1024, 576], P(None, ('dp', 'fsdp')), may hold values from -0.59765625 to 0.59765625
- seg_ids: int32 [2, 32, 1024], P(None, ('dp', 'fsdp')), may hold values from 0 to 7, never falling along the last dimension, each value on 1 to 512 neighbouring positions
- out_grad: bfloat16 [2, 32, 1024, 576], P(None, ('dp', 'fsdp')), may hold values from -6 to 6
- gains: float32 [2, 576], P(None, 'fsdp'), may hold values from 0.5 to 1.5
- matrices: float32 [576, 6144], P('fsdp'), may hold values from -8 to 8
- gain_momentum: float32 [2, 576], P(None, 'fsdp'), may hold values from -0.3 to 0.3
- mat_momentum: float32 [576, 6144], P('fsdp'), may hold values from -0.12 to 0.12
Outputs:
- out_hidden: bfloat16 [2, 32, 1024, 576], P(None, ('dp', 'fsdp'))
- in_grad: float32 [2, 32, 1024, 576], P(None, ('dp', 'fsdp'))
- matrix_grad: float32 [576, 6144], P('fsdp')
- gain_grad: float32 [2, 576], P(None, 'fsdp')
- new_mat_momentum: float32 [576, 6144], P('fsdp')
- new_gain_momentum: float32 [2, 576], P(None, 'fsdp')
- new_matrices: float32 [576, 6144], P('fsdp')
- new_gains: float32 [2, 576], P(None, 'fsdp')
Inputs may be any that keep to these rules, and one draw needn't show every extreme that they name: `seg_ids`: within a sequence segment numbers never fall; a document holds at most 512 tokens.
All inputs are finite; a program needn't handle non-finite values.
Results may differ from a plain program's by a relative error of at most 0.01.
The roundings to bfloat16 on the way count: a program that leaves them out, or rounds other values in their place, can miss the bound.
Values may be sent and summed in bfloat16 or wider, within the bound.
A program may use at most 384 MiB of HBM per device.

v0:
```python
import math
import jax
import jax.numpy as jnp
from jax import lax
from jax.sharding import PartitionSpec as P

D = 576
HEADS = 9
KVH = 3
HD = 64
FF = 1536
QB = 512
NS_STEPS = 5
HIGH = lax.Precision.HIGHEST
EPS_NORM = 1e-05
ROPE_BASE = 100000.0
MOMENT = 0.95
LEARN = 0.05
GAIN_LEARN = 0.1
COEF_A = 3.4445
COEF_B = -4.775
COEF_C = 2.0315
DIMS_ROWS = (((0,), (0,)), ((), ()))
DIMS_COLS = (((1,), (1,)), ((), ()))


def rope_tables(segment):
    seq_len = segment.shape[0]
    token_index = jnp.arange(seq_len, dtype=jnp.int32)
    first_mark = jnp.concatenate([jnp.ones((1,), dtype=bool), segment[1:] != segment[:-1]])
    start_index = lax.cummax(jnp.where(first_mark, token_index, 0), axis=0)
    offset = (token_index - start_index).astype(jnp.float32)
    inverse = 1.0 / ROPE_BASE ** (jnp.arange(0, HD, 2, dtype=jnp.float32) / HD)
    angle = offset[:, None] * inverse[None, :]
    return (jnp.cos(angle)[:, None, :], jnp.sin(angle)[:, None, :])


def rotate(values, cosine, sine):
    half_dim = values.shape[-1] // 2
    first_half = values[..., :half_dim]
    second_half = values[..., half_dim:]
    return jnp.concatenate(
        [first_half * cosine - second_half * sine, second_half * cosine + first_half * sine],
        axis=-1,
    )


def rotate_back(grads, cosine, sine):
    half_dim = grads.shape[-1] // 2
    first_half = grads[..., :half_dim]
    second_half = grads[..., half_dim:]
    return jnp.concatenate(
        [first_half * cosine + second_half * sine, second_half * cosine - first_half * sine],
        axis=-1,
    )


def attention_scores(query_blk, key_rows, segment, start_row, stop_row):
    scores = (
        jnp.einsum("qkgd,tkd->kgqt", query_blk, key_rows, preferred_element_type=jnp.float32)
        * 0.125
    )
    query_pos = start_row + jnp.arange(stop_row - start_row, dtype=jnp.int32)
    key_pos = jnp.arange(stop_row, dtype=jnp.int32)
    allowed = (key_pos[None, :] <= query_pos[:, None]) & (
        segment[:stop_row][None, :] == segment[start_row:stop_row][:, None]
    )
    return (scores, allowed)


def forward_pass(inputs, segment, weights, gain_pair):
    seq_len = inputs.shape[0]
    kv_cols = KVH * HD
    group_size = HEADS // KVH
    block_rows = min(QB, seq_len)
    cosine, sine = rope_tables(segment)
    r_one = lax.rsqrt(jnp.mean(inputs * inputs, axis=-1, keepdims=True) + EPS_NORM)
    u_one = inputs * r_one
    a_low = (u_one * gain_pair[0]).astype(jnp.bfloat16)
    projected = jnp.dot(a_low, weights[:, : D + 2 * kv_cols], preferred_element_type=jnp.float32)
    query_rot = (
        rotate(projected[:, :D].reshape(seq_len, HEADS, HD), cosine, sine)
        .astype(jnp.bfloat16)
        .reshape(seq_len, KVH, group_size, HD)
    )
    key_rot = rotate(projected[:, D : D + kv_cols].reshape(seq_len, KVH, HD), cosine, sine).astype(
        jnp.bfloat16
    )
    value_low = projected[:, D + kv_cols :].astype(jnp.bfloat16).reshape(seq_len, KVH, HD)
    head_out = []
    log_sums = []
    for block_id in range(seq_len // block_rows):
        start_row = block_id * block_rows
        stop_row = start_row + block_rows
        scores, allowed = attention_scores(
            query_rot[start_row:stop_row], key_rot[:stop_row], segment, start_row, stop_row
        )
        scores = jnp.where(allowed, scores, -1e30)
        row_max = jnp.max(scores, axis=-1, keepdims=True)
        exponent = jnp.exp(scores - row_max)
        row_total = jnp.sum(exponent, axis=-1, keepdims=True)
        probs_low = (exponent / row_total).astype(jnp.bfloat16)
        head_out.append(
            jnp.einsum(
                "kgqt,tkd->qkgd",
                probs_low,
                value_low[:stop_row],
                preferred_element_type=jnp.float32,
            ).reshape(block_rows, D)
        )
        log_sums.append(row_max + jnp.log(row_total))
    mixed_low = jnp.concatenate(head_out, axis=0).astype(jnp.bfloat16)
    middle = inputs + jnp.dot(
        mixed_low, weights[:, D + 2 * kv_cols : FF], preferred_element_type=jnp.float32
    )
    r_two = lax.rsqrt(jnp.mean(middle * middle, axis=-1, keepdims=True) + EPS_NORM)
    u_two = middle * r_two
    b_low = (u_two * gain_pair[1]).astype(jnp.bfloat16)
    gate_up = jnp.dot(b_low, weights[:, FF : 3 * FF], preferred_element_type=jnp.float32)
    gate_pre = gate_up[:, :FF]
    up_pre = gate_up[:, FF:]
    inner_low = (jax.nn.silu(gate_pre) * up_pre).astype(jnp.bfloat16)
    result = middle + lax.dot_general(
        inner_low, weights[:, 3 * FF :], DIMS_COLS, preferred_element_type=jnp.float32
    )
    saved = (
        segment,
        cosine,
        sine,
        r_one,
        u_one,
        a_low,
        query_rot,
        key_rot,
        value_low,
        log_sums,
        mixed_low,
        r_two,
        u_two,
        b_low,
        gate_pre,
        up_pre,
        inner_low,
    )
    return (saved, result.astype(jnp.bfloat16))


def backward_pass(saved, cotangent, weights, gain_pair):
    (
        segment,
        cosine,
        sine,
        r_one,
        u_one,
        a_low,
        query_rot,
        key_rot,
        value_low,
        log_sums,
        mixed_low,
        r_two,
        u_two,
        b_low,
        gate_pre,
        up_pre,
        inner_low,
    ) = saved
    seq_len = cotangent.shape[0]
    kv_cols = KVH * HD
    group_size = HEADS // KVH
    block_rows = min(QB, seq_len)
    d_branch = cotangent.astype(jnp.bfloat16)
    grad_down = lax.dot_general(d_branch, inner_low, DIMS_ROWS, preferred_element_type=jnp.float32)
    d_inner = jnp.dot(d_branch, weights[:, 3 * FF :], preferred_element_type=jnp.float32)
    sigma = jax.nn.sigmoid(gate_pre)
    silu_val = gate_pre * sigma
    d_gate = (d_inner * up_pre * sigma * (1.0 + gate_pre * (1.0 - sigma))).astype(jnp.bfloat16)
    d_up = (d_inner * silu_val).astype(jnp.bfloat16)
    d_gate_up = jnp.concatenate([d_gate, d_up], axis=1)
    grad_gate_up = lax.dot_general(b_low, d_gate_up, DIMS_ROWS, preferred_element_type=jnp.float32)
    d_norm_two = lax.dot_general(
        d_gate_up, weights[:, FF : 3 * FF], DIMS_COLS, preferred_element_type=jnp.float32
    )
    grad_gain_two = jnp.sum(d_norm_two * u_two, axis=0)
    d_unit_two = d_norm_two * gain_pair[1]
    d_middle = (
        r_two * (d_unit_two - u_two * jnp.mean(d_unit_two * u_two, axis=-1, keepdims=True))
        + cotangent
    )
    d_attn = d_middle.astype(jnp.bfloat16)
    grad_out = lax.dot_general(mixed_low, d_attn, DIMS_ROWS, preferred_element_type=jnp.float32)
    d_mixed = lax.dot_general(
        d_attn, weights[:, D + 2 * kv_cols : FF], DIMS_COLS, preferred_element_type=jnp.float32
    ).astype(jnp.bfloat16)
    query_grads = []
    d_key = jnp.zeros((seq_len, KVH, HD), jnp.float32)
    d_value = jnp.zeros((seq_len, KVH, HD), jnp.float32)
    for block_id in range(seq_len // block_rows):
        start_row = block_id * block_rows
        stop_row = start_row + block_rows
        query_blk = query_rot[start_row:stop_row]
        scores, allowed = attention_scores(
            query_blk, key_rot[:stop_row], segment, start_row, stop_row
        )
        probs = jnp.where(allowed, jnp.exp(scores - log_sums[block_id]), 0.0)
        probs_low = probs.astype(jnp.bfloat16)
        d_out_blk = d_mixed[start_row:stop_row].reshape(block_rows, KVH, group_size, HD)
        d_probs = jnp.einsum(
            "qkgd,tkd->kgqt", d_out_blk, value_low[:stop_row], preferred_element_type=jnp.float32
        )
        d_scores = (probs * (d_probs - jnp.sum(d_probs * probs, axis=-1, keepdims=True))).astype(
            jnp.bfloat16
        )
        query_grads.append(
            jnp.einsum(
                "kgqt,tkd->qkgd", d_scores, key_rot[:stop_row], preferred_element_type=jnp.float32
            )
            * 0.125
        )
        d_key = d_key.at[:stop_row].add(
            jnp.einsum("kgqt,qkgd->tkd", d_scores, query_blk, preferred_element_type=jnp.float32)
            * 0.125
        )
        d_value = d_value.at[:stop_row].add(
            jnp.einsum("kgqt,qkgd->tkd", probs_low, d_out_blk, preferred_element_type=jnp.float32)
        )
    d_query_rot = jnp.concatenate(query_grads, axis=0).reshape(seq_len, HEADS, HD)
    d_query = rotate_back(d_query_rot, cosine, sine).reshape(seq_len, D)
    d_key_pre = rotate_back(d_key, cosine, sine).reshape(seq_len, kv_cols)
    d_project = jnp.concatenate(
        [d_query, d_key_pre, d_value.reshape(seq_len, kv_cols)], axis=1
    ).astype(jnp.bfloat16)
    grad_project = lax.dot_general(a_low, d_project, DIMS_ROWS, preferred_element_type=jnp.float32)
    d_norm_one = lax.dot_general(
        d_project, weights[:, : D + 2 * kv_cols], DIMS_COLS, preferred_element_type=jnp.float32
    )
    grad_gain_one = jnp.sum(d_norm_one * u_one, axis=0)
    d_unit_one = d_norm_one * gain_pair[0]
    d_input = (
        r_one * (d_unit_one - u_one * jnp.mean(d_unit_one * u_one, axis=-1, keepdims=True))
        + d_middle
    )
    grad_weights = jnp.concatenate([grad_project, grad_out, grad_gate_up, grad_down], axis=1)
    grad_gains = jnp.stack([grad_gain_one, grad_gain_two], axis=0)
    return (d_input, grad_weights, grad_gains)


def orthogonal(matrix):
    tall = matrix.shape[0] > matrix.shape[1]
    work = matrix.T if tall else matrix
    work = work / (jnp.sqrt(jnp.sum(work * work)) + 1e-07)
    for sweep_id in range(NS_STEPS):
        gram = jnp.dot(work, work.T, precision=HIGH)
        poly = COEF_B * gram + COEF_C * jnp.dot(gram, gram, precision=HIGH)
        work = COEF_A * work + jnp.dot(poly, work, precision=HIGH)
    if tall:
        work = work.T
    return work * (0.2 * math.sqrt(max(matrix.shape)))


def attention_block(block):
    kv_cols = KVH * HD
    bounds = [0, D, D + kv_cols, D + 2 * kv_cols, FF]
    pieces = [
        orthogonal(block[:, bounds[block_id] : bounds[block_id + 1]]) for block_id in range(4)
    ]
    return jnp.concatenate(pieces, axis=1)


def feed_block(block):
    return orthogonal(block)


def on_device(hidden_in, seg_ids, out_grad, gains, matrices, gain_momentum, mat_momentum):
    shard_rows = matrices.shape[0]
    total_cols = matrices.shape[1]
    full_rows = shard_rows * lax.axis_size("fsdp")
    total_tokens = (
        hidden_in.shape[0]
        * hidden_in.shape[1]
        * hidden_in.shape[2]
        * lax.axis_size("dp")
        * lax.axis_size("fsdp")
    )
    grad_scale = float(total_tokens) ** (-0.5)
    shard_low = matrices.astype(jnp.bfloat16)
    gain_low = gains.T.astype(jnp.bfloat16)

    def micro_step(running, element):
        inputs, segment, cotangent = element
        weights, gain_rows = (
            lax.all_gather(shard_low, "fsdp", axis=0, tiled=True),
            lax.all_gather(gain_low, "fsdp", axis=0, tiled=True),
        )
        gain_pair = gain_rows.astype(jnp.float32).T
        saved, result = forward_pass(inputs.astype(jnp.float32), segment, weights, gain_pair)
        weights_back, gain_back = (
            lax.all_gather(shard_low, "fsdp", axis=0, tiled=True),
            lax.all_gather(gain_low, "fsdp", axis=0, tiled=True),
        )
        gain_pair_back = gain_back.astype(jnp.float32).T
        d_input, grad_weights, grad_gains = backward_pass(
            saved, cotangent.astype(jnp.float32), weights_back, gain_pair_back
        )
        running = (running[0] + grad_weights, running[1] + grad_gains.T)
        return (running, (result, d_input))

    start_acc = (
        jnp.zeros((full_rows, total_cols), jnp.float32),
        jnp.zeros((full_rows, 2), jnp.float32),
    )
    totals, outputs = lax.scan(
        micro_step, start_acc, (hidden_in[:, 0], seg_ids[:, 0], out_grad[:, 0])
    )
    shard_weights, shard_gains = (
        lax.psum_scatter(totals[0], "fsdp", scatter_dimension=0, tiled=True),
        lax.psum_scatter(totals[1], "fsdp", scatter_dimension=0, tiled=True),
    )
    summed_weights, summed_gains = lax.psum((shard_weights, shard_gains), "dp")
    matrix_grad = summed_weights * grad_scale
    gain_grad = (summed_gains * grad_scale).T
    new_mat_momentum = MOMENT * mat_momentum + matrix_grad
    new_gain_momentum = MOMENT * gain_momentum + gain_grad
    look = matrix_grad + MOMENT * new_mat_momentum
    owner_group = lax.axis_index("dp")
    block_cols = total_cols // 4
    own_block = lax.dynamic_slice_in_dim(look, owner_group * block_cols, block_cols, 1)
    whole_block, whole_gain_mom = (
        lax.all_gather(own_block, "fsdp", axis=0, tiled=True),
        lax.all_gather(new_gain_momentum.T, "fsdp", axis=0, tiled=True),
    )
    orthogonal_block = lax.switch(
        owner_group, [attention_block, feed_block, feed_block, feed_block], whole_block
    )
    own_rows = lax.dynamic_slice_in_dim(
        orthogonal_block, lax.axis_index("fsdp") * shard_rows, shard_rows, 0
    )
    update_rows = lax.all_gather(own_rows, "dp", axis=1, tiled=True)
    new_matrices = matrices - LEARN * update_rows
    spread = lax.rsqrt(jnp.mean(whole_gain_mom * whole_gain_mom, axis=0, keepdims=True) + 1e-06)
    new_gains = gains - GAIN_LEARN * new_gain_momentum * spread.T
    out_hidden = outputs[0][:, None]
    in_grad = outputs[1][:, None]
    return (
        out_hidden,
        in_grad,
        matrix_grad,
        gain_grad,
        new_mat_momentum,
        new_gain_momentum,
        new_matrices,
        new_gains,
    )


def solution(mesh):
    in_specs = (
        P(None, ("dp", "fsdp"), None, None),
        P(None, ("dp", "fsdp"), None),
        P(None, ("dp", "fsdp"), None, None),
        P(None, "fsdp"),
        P("fsdp", None),
        P(None, "fsdp"),
        P("fsdp", None),
    )
    out_specs = (
        P(None, ("dp", "fsdp"), None, None),
        P(None, ("dp", "fsdp"), None, None),
        P("fsdp", None),
        P(None, "fsdp"),
        P("fsdp", None),
        P(None, "fsdp"),
        P("fsdp", None),
        P(None, "fsdp"),
    )
    return jax.shard_map(
        on_device, mesh=mesh, in_specs=in_specs, out_specs=out_specs, check_vma=False
    )
```

profile of v0, /device:TPU:0, one launch (start us, length us, event | category | flops | bytes accessed | tf_op | source)
XLA Modules:
  0.0 1261.2 jit_solution(15243894904164791844)
XLA Ops:
  11.0 648.6 %while.26 = (s32[]{:T(128)}, f32[576,6144]{1,0:T(8,128)}, f32[576,2]{0,1:T(2,128)}, bf16[2,1024,576]{1,2,0:T(8,128)(2,1)}, f32[2,1024,576]{1,2,0:T(8,128)}, /*in...) while((s32[]{:T(128)}, f32[576,6144]{1,0:T(8,128)}, ...), condition=%wide.region_15.16_spmd.clone, body=%wide.region_0.15_spmd.clone.sunk | while | flops 27494117376 | bytes 824622656 | solution.py:312
  12.8 22.6 %all-gather.4 = bf16[8,72,2]{1,2,0:T(2,128)(2,1)S(1)} all-gather(bf16[1,72,2]{1,2,0:T(2,128)(2,1)S(1)} %bitcast.639), channel_id=1, replica_groups=mesh['dp'=4,'fsdp'=8] {'fsdp'}, dimensions={0}, use_global_device_ids=true | all-gather | bytes 2592 | tf_op jit(solution)/shard_map/while/body/eval_jaxpr/all_gather | solution.py:293
  38.7 87.1 %all-gather.13.cloned.1.call-done = bf16[576,6144]{1,0:T(8,128)(2,1)} async-done(((bf16[72,6144]{1,0:T(8,128)(2,1)}), bf16[576,6144]{1,0:T(8,128)(2,1)}) %all-gather.13.cloned.1.call-update) | async-done | bytes 7077904 | tf_op jit(solution)/shard_map/while/body/eval_jaxpr/all_gather | solution.py:292
  148.2 10.2 fusion.692
  159.1 9.4 fusion.693
  171.3 12.0 fusion.698
  183.3 9.8 multiply_convert_fusion.11
  194.8 8.6 fusion.712
  223.5 11.2 fusion.705
  245.4 13.3 %fusion.702 = (f32[3,3,512]{2,1,0:T(4,128)S(1)}, f32[3,1024,512,3]{2,1,3,0:T(8,128)}) fusion(f32[3,1024,512,3]{2,1,3,0:T(8,128)} %get-tuple-element.469, f32[3,3,512]{2,1,0:T(4,128)S(1)} %copy-done.33, pred[512,1024]{0,1:T(8,128)(4,1)S(1)} %fusion.688, bf16[1024,3,64,1]{0,2,3,1:T(8,128)(2,1)S(1)} %bitcast.620, bf16[512,3,3,64]{0,3,2,1:T(8,128)(2,1)S(1)} %bitcast.617), kind=kOutput, calls=%fused_computation.301.clone.1 | convolution fusion | flops 627568128 | bytes 39292928 | tf_op jit(solution)/shard_map/while/body/eval_jaxpr/qkgd,tkd->kgqt/dot_general | solution.py:208
  258.7 8.4 fusion.701
  267.1 13.5 %fusion.703 = bf16[3,3,512,1024]{2,3,1,0:T(8,128)(2,1)S(1)} fusion(f32[3,1024,512,3]{2,1,3,0:T(8,128)} %get-tuple-element.484, f32[3,1024,512,3]{2,1,3,0:T(8,128)} %get-tuple-element.469, f32[3,3,512]{2,1,0:T(4,128)S(1)} %get-tuple-element.485, f32[3,3,512]{2,1,0:T(4,128)S(1)} %copy-done.33, pred[512,1024]{0,1:T(8,128)(4,1)S(1)} %fusion.688), kind=kLoop, calls=%fused_computation.303.clone.1 | loop fusion | flops 28311552 | bytes 47747072 | tf_op jit(solution)/shard_map/while/body/eval_jaxpr/convert_element_type | solution.py:211
  294.7 15.7 %concatenate.101 = f32[576,6144]{1,0:T(8,128)} concatenate(f32[576,960]{1,0:T(8,128)} %fusion.710, f32[576,576]{1,0:T(8,128)} %fusion.711, f32[576,3072]{1,0:T(8,128)} %fusion.712, f32[576,1536]{1,0:T(8,128)} %fusion.713), dimensions={1} | concatenate | bytes 28311552 | tf_op jit(solution)/shard_map/while/body/eval_jaxpr/concatenate | solution.py:243
  310.5 11.6 select_add_fusion.2
  333.2 18.2 %all-gather.4 = bf16[8,72,2]{1,2,0:T(2,128)(2,1)S(1)} all-gather(bf16[1,72,2]{1,2,0:T(2,128)(2,1)S(1)} %bitcast.639), channel_id=1, replica_groups=mesh['dp'=4,'fsdp'=8] {'fsdp'}, dimensions={0}, use_global_device_ids=true | all-gather | bytes 2592 | tf_op jit(solution)/shard_map/while/body/eval_jaxpr/all_gather | solution.py:293
  354.7 86.7 %all-gather.13.cloned.1.call-done = bf16[576,6144]{1,0:T(8,128)(2,1)} async-done(((bf16[72,6144]{1,0:T(8,128)(2,1)}), bf16[576,6144]{1,0:T(8,128)(2,1)}) %all-gather.13.cloned.1.call-update) | async-done | bytes 7077904 | tf_op jit(solution)/shard_map/while/body/eval_jaxpr/all_gather | solution.py:292
  463.6 10.2 fusion.692
  474.5 9.4 fusion.693
  486.7 11.4 fusion.698
  498.1 9.8 multiply_convert_fusion.11
  509.7 8.6 fusion.712
  538.6 11.2 fusion.705
  560.5 13.3 %fusion.702 = (f32[3,3,512]{2,1,0:T(4,128)S(1)}, f32[3,1024,512,3]{2,1,3,0:T(8,128)}) fusion(f32[3,1024,512,3]{2,1,3,0:T(8,128)} %get-tuple-element.469, f32[3,3,512]{2,1,0:T(4,128)S(1)} %copy-done.33, pred[512,1024]{0,1:T(8,128)(4,1)S(1)} %fusion.688, bf16[1024,3,64,1]{0,2,3,1:T(8,128)(2,1)S(1)} %bitcast.620, bf16[512,3,3,64]{0,3,2,1:T(8,128)(2,1)S(1)} %bitcast.617), kind=kOutput, calls=%fused_computation.301.clone.1 | convolution fusion | flops 627568128 | bytes 39292928 | tf_op jit(solution)/shard_map/while/body/eval_jaxpr/qkgd,tkd->kgqt/dot_general | solution.py:208
  582.2 13.5 %fusion.703 = bf16[3,3,512,1024]{2,3,1,0:T(8,128)(2,1)S(1)} fusion(f32[3,1024,512,3]{2,1,3,0:T(8,128)} %get-tuple-element.484, f32[3,1024,512,3]{2,1,3,0:T(8,128)} %get-tuple-element.469, f32[3,3,512]{2,1,0:T(4,128)S(1)} %get-tuple-element.485, f32[3,3,512]{2,1,0:T(4,128)S(1)} %copy-done.33, pred[512,1024]{0,1:T(8,128)(4,1)S(1)} %fusion.688), kind=kLoop, calls=%fused_computation.303.clone.1 | loop fusion | flops 28311552 | bytes 47747072 | tf_op jit(solution)/shard_map/while/body/eval_jaxpr/convert_element_type | solution.py:211
  609.8 15.7 %concatenate.101 = f32[576,6144]{1,0:T(8,128)} concatenate(f32[576,960]{1,0:T(8,128)} %fusion.710, f32[576,576]{1,0:T(8,128)} %fusion.711, f32[576,3072]{1,0:T(8,128)} %fusion.712, f32[576,1536]{1,0:T(8,128)} %fusion.713), dimensions={1} | concatenate | bytes 28311552 | tf_op jit(solution)/shard_map/while/body/eval_jaxpr/concatenate | solution.py:243
  625.6 15.6 %select_add_fusion.2 = f32[576,6144]{1,0:T(8,128)} fusion(f32[576,6144]{1,0:T(8,128)} %concatenate.101, f32[576,6144]{1,0:T(8,128)} %get-tuple-element.514, pred[]{:T(512)S(6)} %compare.47), kind=kLoop, calls=%fused_computation.312.clone.1 | loop fusion | flops 7077888 | bytes 42467328 | tf_op jit(solution)/shard_map/while/body/eval_jaxpr/add | solution.py:305
  660.3 231.0 %reduce-scatter.3.cloned.1.call-done = f32[72,6144]{1,0:T(8,128)} async-done(((f32[576,6144]{1,0:T(8,128)}), f32[72,6144]{1,0:T(8,128)}) %reduce-scatter.3.cloned.1.call-update) | async-done | bytes 1769488 | tf_op jit(solution)/shard_map/reduce_scatter | solution.py:316
  891.4 47.2 %all-reduce.5.cloned.1.call-done = f32[72,6144]{1,0:T(8,128)} async-done(((f32[72,6144]{1,0:T(8,128)}), f32[72,6144]{1,0:T(8,128)}) %all-reduce.5.cloned.1.call-update) | async-done | bytes 1769488 | tf_op jit(solution)/shard_map/psum | solution.py:319
  943.1 64.5 %all-gather.9.cloned.1.call-done = f32[576,1536]{1,0:T(8,128)} async-done(((f32[72,1536]{1,0:T(8,128)}), f32[576,1536]{1,0:T(8,128)}) %all-gather.9.cloned.1.call-update) | async-done | bytes 3538960 | tf_op jit(solution)/shard_map/all_gather | solution.py:329
  1007.6 196.8 %conditional.1 = (f32[576,1536]{1,0:T(8,128)S(1)}) conditional(s32[]{:T(128)} %clamp.3, f32[576,1536]{1,0:T(8,128)} %all-gather.9.cloned.1.call-done, f32[576,1536]{1,0:T(8,128)} %all-gather.9.cloned.1.call-done, f32[576,1536]{1,0:T(8,128)} %all-gather.9.cloned.1.call-done, ...), branch_computations={%region_20.25_spmd, %region_25.27_spmd, %region_27.29_spmd, %regio... | conditional | flops 74772799488 | bytes 174001792 | solution.py:332
  1207.2 19.4 %all-reduce.2 = f32[576,2]{0,1:T(2,128)S(1)} all-reduce(f32[576,2]{0,1:T(2,128)S(1)} %copy-done.47), channel_id=3, replica_groups=mesh['dp'=4,'fsdp'=8] {'fsdp'}, use_global_device_ids=true, to_apply=%region_18.19.clone | all-reduce | flops 1152 | bytes 9216
  1233.0 16.3 %all-gather.1 = f32[8,72,2]{1,2,0:T(2,128)S(1)} all-gather(f32[1,72,2]{1,2,0:T(2,128)S(1)} %bitcast.640), channel_id=1, replica_groups=mesh['dp'=4,'fsdp'=8] {'fsdp'}, dimensions={0}, use_global_device_ids=true | all-gather | bytes 5184 | tf_op jit(solution)/shard_map/all_gather | solution.py:330
  (449 shorter events, 367.1 us)
Async XLA Ops:
  11.3 26.1 %copy-start.43 = (s32[2,1024]{1,0:T(2,128)}, s32[2,1024]{1,0:T(2,128)S(1)}, u32[]{:S(2)}) copy-start(s32[2,1024]{1,0:T(2,128)S(1)} %get-tuple-element.537) | copy-start | bytes 24580 | tf_op jit(solution)/shard_map/while
  11.3 114.5 %all-gather.13.cloned.1.call-start = ((), (), s32[]{:S(2)}) async-start(), calls=%async_computation.5 | async-start | bytes 7962624 | tf_op jit(solution)/shard_map/while/body/eval_jaxpr/all_gather | solution.py:292
  37.3 92.0 %copy-start.41 = (f32[576]{0:T(1024)}, f32[576]{0:T(1024)S(1)}, u32[]{:S(2)}) copy-start(f32[576]{0:T(1024)S(1)} %get-tuple-element.458) | copy-start | bytes 6916 | tf_op jit(solution)/shard_map/while
  37.3 92.0 %copy-start.34 = (f32[1024]{0:T(1024)}, f32[1024]{0:T(1024)S(1)}, u32[]{:S(2)}) copy-start(f32[1024]{0:T(1024)S(1)} %add_rsqrt_fusion.4) | copy-start | bytes 12292 | tf_op jit(solution)/shard_map/while
  38.2 92.6 %copy-start.6 = (f32[1024,32]{0,1:T(8,128)}, f32[1024,32]{0,1:T(8,128)S(1)}, u32[]{:S(2)}) copy-start(f32[1024,32]{0,1:T(8,128)S(1)} %get-tuple-element.463) | copy-start | bytes 393220 | tf_op jit(solution)/shard_map/while
  38.2 92.6 %copy-start.8 = (f32[1024,32]{0,1:T(8,128)}, f32[1024,32]{0,1:T(8,128)S(1)}, u32[]{:S(2)}) copy-start(f32[1024,32]{0,1:T(8,128)S(1)} %get-tuple-element.462) | copy-start | bytes 393220 | tf_op jit(solution)/shard_map/while
  168.5 14.8 %slice-start.3 = ((s8[7077888]{0:T(1024)(128)(4,1)}), s8[4194304]{0:T(1024)(128)(4,1)S(1)}, s32[]{:S(2)}) async-start(s8[7077888]{0:T(1024)(128)(4,1)} %bitcast.632), calls=%async_computation.9 | async-start | bytes 8388608 | tf_op jit(solution)/shard_map/while
  171.2 38.8 %copy-start.18 = (f32[1024,576]{0,1:T(8,128)}, f32[1024,576]{0,1:T(8,128)S(1)}, u32[]{:S(2)}) copy-start(f32[1024,576]{0,1:T(8,128)S(1)} %get-tuple-element.475) | copy-start | bytes 7077892 | tf_op jit(solution)/shard_map/while
  171.2 12.0 copy-start.29
  171.3 12.0 slice-start.4
  245.4 13.3 %copy-start.57 = (f32[512,3,64]{0,2,1:T(8,128)S(1)}, f32[512,3,64]{0,2,1:T(8,128)}, u32[]{:S(2)}) copy-start(f32[512,3,64]{0,2,1:T(8,128)} %fusion.700) | copy-start | bytes 1179652 | tf_op jit(solution)/shard_map/while
  331.7 21.8 %copy-start.43 = (s32[2,1024]{1,0:T(2,128)}, s32[2,1024]{1,0:T(2,128)S(1)}, u32[]{:S(2)}) copy-start(s32[2,1024]{1,0:T(2,128)S(1)} %get-tuple-element.537) | copy-start | bytes 24580 | tf_op jit(solution)/shard_map/while
  331.7 109.7 %all-gather.13.cloned.1.call-start = ((), (), s32[]{:S(2)}) async-start(), calls=%async_computation.5 | async-start | bytes 7962624 | tf_op jit(solution)/shard_map/while/body/eval_jaxpr/all_gather | solution.py:292
  353.4 91.5 %copy-start.41 = (f32[576]{0:T(1024)}, f32[576]{0:T(1024)S(1)}, u32[]{:S(2)}) copy-start(f32[576]{0:T(1024)S(1)} %get-tuple-element.458) | copy-start | bytes 6916 | tf_op jit(solution)/shard_map/while
  353.4 91.5 %copy-start.34 = (f32[1024]{0:T(1024)}, f32[1024]{0:T(1024)S(1)}, u32[]{:S(2)}) copy-start(f32[1024]{0:T(1024)S(1)} %add_rsqrt_fusion.4) | copy-start | bytes 12292 | tf_op jit(solution)/shard_map/while
  354.2 92.1 %copy-start.6 = (f32[1024,32]{0,1:T(8,128)}, f32[1024,32]{0,1:T(8,128)S(1)}, u32[]{:S(2)}) copy-start(f32[1024,32]{0,1:T(8,128)S(1)} %get-tuple-element.463) | copy-start | bytes 393220 | tf_op jit(solution)/shard_map/while
  354.2 92.1 %copy-start.8 = (f32[1024,32]{0,1:T(8,128)}, f32[1024,32]{0,1:T(8,128)S(1)}, u32[]{:S(2)}) copy-start(f32[1024,32]{0,1:T(8,128)S(1)} %get-tuple-element.462) | copy-start | bytes 393220 | tf_op jit(solution)/shard_map/while
  483.9 14.2 %slice-start.3 = ((s8[7077888]{0:T(1024)(128)(4,1)}), s8[4194304]{0:T(1024)(128)(4,1)S(1)}, s32[]{:S(2)}) async-start(s8[7077888]{0:T(1024)(128)(4,1)} %bitcast.632), calls=%async_computation.9 | async-start | bytes 8388608 | tf_op jit(solution)/shard_map/while
  486.7 38.5 %copy-start.18 = (f32[1024,576]{0,1:T(8,128)}, f32[1024,576]{0,1:T(8,128)S(1)}, u32[]{:S(2)}) copy-start(f32[1024,576]{0,1:T(8,128)S(1)} %get-tuple-element.475) | copy-start | bytes 7077892 | tf_op jit(solution)/shard_map/while
  560.5 13.3 %copy-start.57 = (f32[512,3,64]{0,2,1:T(8,128)S(1)}, f32[512,3,64]{0,2,1:T(8,128)}, u32[]{:S(2)}) copy-start(f32[512,3,64]{0,2,1:T(8,128)} %fusion.700) | copy-start | bytes 1179652 | tf_op jit(solution)/shard_map/while
  625.6 15.6 %copy-start.45 = (f32[576,2]{0,1:T(2,128)S(1)}, f32[576,2]{0,1:T(2,128)}, u32[]{:S(2)}) copy-start(f32[576,2]{0,1:T(2,128)} %get-tuple-element.515) | copy-start | bytes 13828 | tf_op jit(solution)/shard_map/while
  625.6 15.6 %copy-start.4 = (bf16[2,1024,576]{1,2,0:T(8,128)(2,1)S(1)}, bf16[2,1024,576]{1,2,0:T(8,128)(2,1)}, u32[]{:S(2)}) copy-start(bf16[2,1024,576]{1,2,0:T(8,128)(2,1)} %get-tuple-element.534) | copy-start | bytes 7077892 | tf_op jit(solution)/shard_map/while
  625.6 15.6 %copy-start.20 = (f32[1024,576]{0,1:T(8,128)S(1)}, f32[1024,576]{0,1:T(8,128)}, u32[]{:S(2)}) copy-start(f32[1024,576]{0,1:T(8,128)} %get-tuple-element.495) | copy-start | bytes 7077892 | tf_op jit(solution)/shard_map/while
  659.6 231.7 %reduce-scatter.3.cloned.1.call-start = ((), (), s32[]{:S(2)}) async-start(), calls=%async_computation.1 | async-start | bytes 15925248 | tf_op jit(solution)/shard_map/reduce_scatter | solution.py:316
  660.2 278.4 %copy-start.40 = (f32[72,6144]{1,0:T(8,128)S(1)}, f32[72,6144]{1,0:T(8,128)}, u32[]{:S(2)}) copy-start(f32[72,6144]{1,0:T(8,128)} %param.31) | copy-start | bytes 5308420
  660.2 278.4 %all-reduce.5.cloned.1.call-start = ((), (), s32[]{:S(2)}) async-start(), calls=%async_computation.2 | async-start | bytes 3538944 | tf_op jit(solution)/shard_map/psum | solution.py:319
  891.3 116.3 %all-gather.9.cloned.1.call-start = ((), (), s32[]{:S(2)}) async-start(), calls=%async_computation.3 | async-start | bytes 3981312 | tf_op jit(solution)/shard_map/all_gather | solution.py:329
  943.0 307.0 %all-gather.11.cloned.1.call-start = ((), (), s32[]{:S(2)}) async-start(), calls=%async_computation.4 | async-start | bytes 2211840 | tf_op jit(solution)/shard_map/all_gather | solution.py:338
  1007.6 199.6 %copy-start.47 = (f32[576,2]{0,1:T(2,128)S(1)}, f32[576,2]{0,1:T(2,128)}, u32[]{:S(2)}) copy-start(f32[576,2]{0,1:T(2,128)} %get-tuple-element.254) | copy-start | bytes 13828
  1007.6 224.8 %copy-start.52 = (f32[2,72]{1,0:T(2,128)S(1)}, f32[2,72]{1,0:T(2,128)}, u32[]{:S(2)}) copy-start(f32[2,72]{1,0:T(2,128)} %param.30) | copy-start | bytes 1732
  1007.6 241.8 %copy-start.51 = (f32[2,72]{1,0:T(2,128)S(1)}, f32[2,72]{1,0:T(2,128)}, u32[]{:S(2)}) copy-start(f32[2,72]{1,0:T(2,128)} %param.28) | copy-start | bytes 1732
  1233.0 20.5 %copy-start.50 = (f32[2,72]{1,0:T(2,128)}, f32[2,72]{1,0:T(2,128)S(1)}, u32[]{:S(2)}) copy-start(f32[2,72]{1,0:T(2,128)S(1)} %get-tuple-element.318) | copy-start | bytes 1732
  (88 other events, 430.6 us)
Sparse Core Ops, SparseCore 0:
  14.9 110.8 all-gather.12
  335.3 106.0 all-gather.12
Sparse Core Ops, SparseCore 1:
  663.8 227.5 reduce-scatter.2
  893.6 45.0 all-reduce.4
  943.1 64.4 all-gather.8
  1205.4 18.4 all-gather.10
where the time goes:
time: 1260 us
  waiting for transfers between devices  517 us (41%)
  matrix products  405 us (32%)
  other arithmetic  134 us (11%)
  blocking collectives  82.2 us (7%)
  local copies, waits for them, and re-layouts  63.8 us (5%)
  loops' own time  42.1 us (3%)
  between operations  16.6 us (1%)
    reduce_scatter x1, waiting for transfers between devices, on_device(): lax.psum_scatter(totals[0], 'fsdp', scatter_dimension=0, tiled=True)  231 us
    all_gather x2, waiting for transfers between devices, micro_step(): lax.all_gather(shard_low, 'fsdp', axis=0, tiled=True)  174 us
    all_gather x1, waiting for transfers between devices, on_device(): lax.all_gather(own_block, 'fsdp', axis=0, tiled=True)  64.5 us
    dot_general x20, matrix products, orthogonal(): gram = jnp.dot(work, work.T, precision=HIGH)  56.5 us
    dot_general x20, matrix products, orthogonal(): work = COEF_A * work + jnp.dot(poly, work, precision=HIGH)  54.7 us
    convert_element_type x4, other arithmetic, backward_pass(): (probs * (d_probs - jnp.sum(d_probs * probs, axis=-1, keepdims=True))).as...  49.4 us
    psum x1, waiting for transfers between devices, on_device(): summed_weights, summed_gains = lax.psum((shard_weights, shard_gains), 'dp')  47.2 us
    dot_general x20, matrix products, orthogonal(): poly = COEF_B * gram + COEF_C * jnp.dot(gram, gram, precision=HIGH)  46.2 us
  transfers between devices with their start and end apart: 6, of which 5 were waited for; matrix products, arithmetic and copies ran while one was open for 1% of the time, Pallas kernels for 0%

commit v1 on v0

--- a/solution.py
+++ b/solution.py
@@ -289,7 +289,9 @@
     def micro_step(running, element):
         inputs, segment, cotangent = element
         weights, gain_rows = (
-            lax.all_gather(shard_low, "fsdp", axis=0, tiled=True),
+            jnp.concatenate(
+                lax.all_to_all(jnp.stack([shard_low] * lax.axis_size("fsdp")), "fsdp", 0, 0), axis=0
+            ),
             lax.all_gather(gain_low, "fsdp", axis=0, tiled=True),
         )
         gain_pair = gain_rows.astype(jnp.float32).T

time: 1260 us -> 1570 us (1.25)
  blocking collectives: 82.2 us -> 396 us
  waiting for transfers between devices: 517 us -> 469 us
  starting transfers between devices: 0.26 us -> 24.3 us
  local copies, waits for them, and re-layouts: 63.8 us -> 80.6 us
    all_gather x2, blocking collectives: 40.8 us -> 354 us  [micro_step(): lax.all_gather(gain_low, 'fsdp', axis=0, tiled=True)]
    all_gather x2, waiting for transfers between devices: 174 us -> 0.01 us  [micro_step(): lax.all_gather(shard_low, 'fsdp', axis=0, tiled=True)]
    all_to_all x0 -> x2, waiting for transfers between devices: none -> 110 us  [micro_step(): lax.all_to_all(jnp.stack([shard_low] * lax.axis_size('fsdp')), 'fsdp', 0, 0)]
    all_to_all x0 -> x2, starting transfers between devices: none -> 24.1 us  [micro_step(): lax.all_to_all(jnp.stack([shard_low] * lax.axis_size('fsdp')), 'fsdp', 0, 0)]
  transfers between devices with their start and end apart: 6 -> 8, of which waited for: 5 -> 5; matrix products, arithmetic and copies ran while one was open for 1% -> 8% of each run, Pallas kernels for 0% -> 0%
where the time goes in v1:
time: 1570 us
  waiting for transfers between devices  469 us (30%)
  matrix products  399 us (25%)
  blocking collectives  396 us (25%)
  other arithmetic  141 us (9%)
  local copies, waits for them, and re-layouts  80.6 us (5%)
  loops' own time  42.2 us (3%)
  starting transfers between devices  24.3 us (2%)
  between operations  16.7 us (1%)
    all_gather x2, blocking collectives, micro_step(): lax.all_gather(gain_low, 'fsdp', axis=0, tiled=True)  354 us
    reduce_scatter x1, waiting for transfers between devices, on_device(): lax.psum_scatter(totals[0], 'fsdp', scatter_dimension=0, tiled=True)  245 us
    all_to_all x2, waiting for transfers between devices, micro_step(): lax.all_to_all(jnp.stack([shard_low] * lax.axis_size('fsdp')), 'fsdp', 0, 0)  110 us
    all_gather x1, waiting for transfers between devices, on_device(): lax.all_gather(own_block, 'fsdp', axis=0, tiled=True)  64.5 us
    dot_general x20, matrix products, orthogonal(): gram = jnp.dot(work, work.T, precision=HIGH)  56.9 us
    dot_general x20, matrix products, orthogonal(): work = COEF_A * work + jnp.dot(poly, work, precision=HIGH)  54.7 us
    convert_element_type x4, other arithmetic, backward_pass(): (probs * (d_probs - jnp.sum(d_probs * probs, axis=-1, keepdims=True))).as...  49.6 us
    psum x1, waiting for transfers between devices, on_device(): summed_weights, summed_gains = lax.psum((shard_weights, shard_gains), 'dp')  47.2 us
  transfers between devices with their start and end apart: 8, of which 5 were waited for; matrix products, arithmetic and copies ran while one was open for 8% of the time, Pallas kernels for 0%

profile of v1, /device:TPU:0, one launch (start us, length us, event | category | flops | bytes accessed | tf_op | source)
XLA Modules:
  0.0 1569.0 jit_solution(17242305922069696648)
XLA Ops:
  13.0 940.8 %while.26 = (s32[]{:T(128)}, f32[576,6144]{1,0:T(8,128)}, f32[576,2]{0,1:T(2,128)}, bf16[2,1024,576]{1,2,0:T(8,128)(2,1)}, f32[2,1024,576]{1,2,0:T(8,128)}, /*in...) while((s32[]{:T(128)}, f32[576,6144]{1,0:T(8,128)}, ...), condition=%wide.region_15.16_spmd.clone, body=%wide.region_0.15_spmd.clone.sunk | while | flops 27494117376 | bytes 895872512 | solution.py:314
  27.4 177.9 %all-gather.4 = bf16[8,72,2]{1,2,0:T(2,128)(2,1)S(1)} all-gather(bf16[1,72,2]{1,2,0:T(2,128)(2,1)} %bitcast.589), channel_id=1, replica_groups=mesh['dp'=4,'fsdp'=8] {'fsdp'}, dimensions={0}, use_global_device_ids=true | all-gather | bytes 2592 | tf_op jit(solution)/shard_map/while/body/eval_jaxpr/all_gather | solution.py:295
  210.4 55.9 %all-to-all-done = bf16[8,72,6144]{2,1,0:T(8,128)(2,1)} async-done(((bf16[8,72,6144]{2,1,0:T(8,128)(2,1)}), bf16[8,72,6144]{2,1,0:T(8,128)(2,1)}, u32[]{:S(2)}, u32[]{:S(2)}) %all-to-all-start) | async-done | bytes 7077920 | tf_op jit(solution)/shard_map/while/body/eval_jaxpr/all_to_all | solution.py:293
  277.5 8.2 fusion.691
  285.7 10.3 fusion.692
  315.6 10.4 fusion.698
  326.0 10.7 multiply_convert_fusion.11
  366.6 11.2 fusion.705
  393.5 13.2 fusion.702
  406.7 8.4 fusion.701
  415.1 13.6 fusion.703
  443.5 15.8 %concatenate.101 = f32[576,6144]{1,0:T(8,128)} concatenate(f32[576,960]{1,0:T(8,128)} %fusion.710, f32[576,576]{1,0:T(8,128)} %fusion.711, f32[576,3072]{1,0:T(8,128)} %fusion.712, f32[576,1536]{1,0:T(8,128)} %fusion.713), dimensions={1} | concatenate | bytes 28311552 | tf_op jit(solution)/shard_map/while/body/eval_jaxpr/concatenate | solution.py:243
  459.3 10.8 select_add_fusion.2
  478.7 16.8 %all-to-all-start = ((bf16[8,72,6144]{2,1,0:T(8,128)(2,1)}), bf16[8,72,6144]{2,1,0:T(8,128)(2,1)}, u32[]{:S(2)}, u32[]{:S(2)}) async-start(bf16[8,72,6144]{2,1,0:T(8,128)(2,1)} %stack.39), calls=%async_computation | async-start | bytes 14155776 | tf_op jit(solution)/shard_map/while/body/eval_jaxpr/all_to_all | solution.py:293
  497.1 176.4 %all-gather.4 = bf16[8,72,2]{1,2,0:T(2,128)(2,1)S(1)} all-gather(bf16[1,72,2]{1,2,0:T(2,128)(2,1)} %bitcast.589), channel_id=1, replica_groups=mesh['dp'=4,'fsdp'=8] {'fsdp'}, dimensions={0}, use_global_device_ids=true | all-gather | bytes 2592 | tf_op jit(solution)/shard_map/while/body/eval_jaxpr/all_gather | solution.py:295
  678.5 54.6 %all-to-all-done = bf16[8,72,6144]{2,1,0:T(8,128)(2,1)} async-done(((bf16[8,72,6144]{2,1,0:T(8,128)(2,1)}), bf16[8,72,6144]{2,1,0:T(8,128)(2,1)}, u32[]{:S(2)}, u32[]{:S(2)}) %all-to-all-start) | async-done | bytes 7077920 | tf_op jit(solution)/shard_map/while/body/eval_jaxpr/all_to_all | solution.py:293
  744.2 8.2 fusion.691
  752.4 10.3 fusion.692
  782.4 10.4 fusion.698
  792.8 10.7 multiply_convert_fusion.11
  833.4 11.2 fusion.705
  860.3 13.2 fusion.702
  873.5 8.4 fusion.701
  881.9 13.6 fusion.703
  910.3 15.8 %concatenate.101 = f32[576,6144]{1,0:T(8,128)} concatenate(f32[576,960]{1,0:T(8,128)} %fusion.710, f32[576,576]{1,0:T(8,128)} %fusion.711, f32[576,3072]{1,0:T(8,128)} %fusion.712, f32[576,1536]{1,0:T(8,128)} %fusion.713), dimensions={1} | concatenate | bytes 28311552 | tf_op jit(solution)/shard_map/while/body/eval_jaxpr/concatenate | solution.py:243
  926.0 15.2 select_add_fusion.2
  954.5 244.7 %reduce-scatter.3.cloned.1.call-done = f32[72,6144]{1,0:T(8,128)} async-done(((f32[576,6144]{1,0:T(8,128)}), f32[72,6144]{1,0:T(8,128)}) %reduce-scatter.3.cloned.1.call-update) | async-done | bytes 1769488 | tf_op jit(solution)/shard_map/reduce_scatter | solution.py:318
  1199.2 47.2 %all-reduce.5.cloned.1.call-done = f32[72,6144]{1,0:T(8,128)} async-done(((f32[72,6144]{1,0:T(8,128)}), f32[72,6144]{1,0:T(8,128)}) %all-reduce.5.cloned.1.call-update) | async-done | bytes 1769488 | tf_op jit(solution)/shard_map/psum | solution.py:321
  1250.9 64.5 %all-gather.9.cloned.1.call-done = f32[576,1536]{1,0:T(8,128)} async-done(((f32[72,1536]{1,0:T(8,128)}), f32[576,1536]{1,0:T(8,128)}) %all-gather.9.cloned.1.call-update) | async-done | bytes 3538960 | tf_op jit(solution)/shard_map/all_gather | solution.py:331
  1315.4 196.8 %conditional.1 = (f32[576,1536]{1,0:T(8,128)S(1)}) conditional(s32[]{:T(128)} %clamp.3, f32[576,1536]{1,0:T(8,128)} %all-gather.9.cloned.1.call-done, f32[576,1536]{1,0:T(8,128)} %all-gather.9.cloned.1.call-done, f32[576,1536]{1,0:T(8,128)} %all-gather.9.cloned.1.call-done, ...), branch_computations={%region_20.25_spmd, %region_25.27_spmd, %region_27.29_spmd, %regio... | conditional | flops 74772799488 | bytes 174001792 | solution.py:334
  1514.9 19.4 %all-reduce.2 = f32[576,2]{0,1:T(2,128)S(1)} all-reduce(f32[576,2]{0,1:T(2,128)S(1)} %copy-done.50), channel_id=3, replica_groups=mesh['dp'=4,'fsdp'=8] {'fsdp'}, use_global_device_ids=true, to_apply=%region_18.19.clone | all-reduce | flops 1152 | bytes 9216
  1540.7 16.3 %all-gather.1 = f32[8,72,2]{1,2,0:T(2,128)S(1)} all-gather(f32[1,72,2]{1,2,0:T(2,128)S(1)} %bitcast.638), channel_id=1, replica_groups=mesh['dp'=4,'fsdp'=8] {'fsdp'}, dimensions={0}, use_global_device_ids=true | all-gather | bytes 5184 | tf_op jit(solution)/shard_map/all_gather | solution.py:332
  (449 shorter events, 407.0 us)
Async XLA Ops:
  18.5 247.9 %all-to-all-start = ((bf16[8,72,6144]{2,1,0:T(8,128)(2,1)}), bf16[8,72,6144]{2,1,0:T(8,128)(2,1)}, u32[]{:S(2)}, u32[]{:S(2)}) async-start(bf16[8,72,6144]{2,1,0:T(8,128)(2,1)} %stack.39), calls=%async_computation | async-start | bytes 14155776 | tf_op jit(solution)/shard_map/while/body/eval_jaxpr/all_to_all | solution.py:293
  25.7 300.3 %all-gather.13.cloned.1.call-start = ((), (), s32[]{:S(2)}) async-start(), calls=%async_computation.6 | async-start | bytes 7962624 | tf_op jit(solution)/shard_map/while/body/eval_jaxpr/all_gather | solution.py:300
  209.0 60.8 %copy-start.46 = (f32[576]{0:T(1024)}, f32[576]{0:T(1024)S(1)}, u32[]{:S(2)}) copy-start(f32[576]{0:T(1024)S(1)} %get-tuple-element.458) | copy-start | bytes 6916 | tf_op jit(solution)/shard_map/while
  209.0 60.7 %copy-start.35 = (f32[1024]{0:T(1024)}, f32[1024]{0:T(1024)S(1)}, u32[]{:S(2)}) copy-start(f32[1024]{0:T(1024)S(1)} %add_rsqrt_fusion.4) | copy-start | bytes 12292 | tf_op jit(solution)/shard_map/while
  209.9 62.1 %copy-start.4 = (f32[1024,32]{0,1:T(8,128)}, f32[1024,32]{0,1:T(8,128)S(1)}, u32[]{:S(2)}) copy-start(f32[1024,32]{0,1:T(8,128)S(1)} %get-tuple-element.463) | copy-start | bytes 393220 | tf_op jit(solution)/shard_map/while
  209.9 62.1 %copy-start.6 = (f32[1024,32]{0,1:T(8,128)}, f32[1024,32]{0,1:T(8,128)S(1)}, u32[]{:S(2)}) copy-start(f32[1024,32]{0,1:T(8,128)S(1)} %get-tuple-element.462) | copy-start | bytes 393220 | tf_op jit(solution)/shard_map/while
  273.8 22.1 %copy-start.32 = (f32[3,3,512]{2,1,0:T(4,128)}, f32[3,3,512]{2,1,0:T(4,128)S(1)}, u32[]{:S(2)}) copy-start(f32[3,3,512]{2,1,0:T(4,128)S(1)} %get-tuple-element.474) | copy-start | bytes 55300 | tf_op jit(solution)/shard_map/while
  277.4 18.5 %copy-start.39 = (f32[3,3,512]{2,1,0:T(4,128)}, f32[3,3,512]{2,1,0:T(4,128)S(1)}, u32[]{:S(2)}) copy-start(f32[3,3,512]{2,1,0:T(4,128)S(1)} %fusion.696) | copy-start | bytes 55300 | tf_op jit(solution)/shard_map/while
  285.7 15.8 %copy-start.41 = (f32[3,3,512]{2,1,0:T(4,128)}, f32[3,3,512]{2,1,0:T(4,128)S(1)}, u32[]{:S(2)}) copy-start(f32[3,3,512]{2,1,0:T(4,128)S(1)} %get-tuple-element.470) | copy-start | bytes 55300 | tf_op jit(solution)/shard_map/while
  314.2 30.7 %copy-start.16 = (f32[1024,576]{0,1:T(8,128)}, f32[1024,576]{0,1:T(8,128)S(1)}, u32[]{:S(2)}) copy-start(f32[1024,576]{0,1:T(8,128)S(1)} %get-tuple-element.475) | copy-start | bytes 7077892 | tf_op jit(solution)/shard_map/while
  393.5 13.2 copy-start.58
  478.7 254.4 %all-to-all-start = ((bf16[8,72,6144]{2,1,0:T(8,128)(2,1)}), bf16[8,72,6144]{2,1,0:T(8,128)(2,1)}, u32[]{:S(2)}, u32[]{:S(2)}) async-start(bf16[8,72,6144]{2,1,0:T(8,128)(2,1)} %stack.39), calls=%async_computation | async-start | bytes 14155776 | tf_op jit(solution)/shard_map/while/body/eval_jaxpr/all_to_all | solution.py:293
  495.5 297.4 %all-gather.13.cloned.1.call-start = ((), (), s32[]{:S(2)}) async-start(), calls=%async_computation.6 | async-start | bytes 7962624 | tf_op jit(solution)/shard_map/while/body/eval_jaxpr/all_gather | solution.py:300
  677.2 59.4 %copy-start.46 = (f32[576]{0:T(1024)}, f32[576]{0:T(1024)S(1)}, u32[]{:S(2)}) copy-start(f32[576]{0:T(1024)S(1)} %get-tuple-element.458) | copy-start | bytes 6916 | tf_op jit(solution)/shard_map/while
  677.2 59.4 %copy-start.35 = (f32[1024]{0:T(1024)}, f32[1024]{0:T(1024)S(1)}, u32[]{:S(2)}) copy-start(f32[1024]{0:T(1024)S(1)} %add_rsqrt_fusion.4) | copy-start | bytes 12292 | tf_op jit(solution)/shard_map/while
  678.0 60.8 %copy-start.4 = (f32[1024,32]{0,1:T(8,128)}, f32[1024,32]{0,1:T(8,128)S(1)}, u32[]{:S(2)}) copy-start(f32[1024,32]{0,1:T(8,128)S(1)} %get-tuple-element.463) | copy-start | bytes 393220 | tf_op jit(solution)/shard_map/while
  678.0 60.8 %copy-start.6 = (f32[1024,32]{0,1:T(8,128)}, f32[1024,32]{0,1:T(8,128)S(1)}, u32[]{:S(2)}) copy-start(f32[1024,32]{0,1:T(8,128)S(1)} %get-tuple-element.462) | copy-start | bytes 393220 | tf_op jit(solution)/shard_map/while
  740.6 22.1 %copy-start.32 = (f32[3,3,512]{2,1,0:T(4,128)}, f32[3,3,512]{2,1,0:T(4,128)S(1)}, u32[]{:S(2)}) copy-start(f32[3,3,512]{2,1,0:T(4,128)S(1)} %get-tuple-element.474) | copy-start | bytes 55300 | tf_op jit(solution)/shard_map/while
  744.2 18.5 %copy-start.39 = (f32[3,3,512]{2,1,0:T(4,128)}, f32[3,3,512]{2,1,0:T(4,128)S(1)}, u32[]{:S(2)}) copy-start(f32[3,3,512]{2,1,0:T(4,128)S(1)} %fusion.696) | copy-start | bytes 55300 | tf_op jit(solution)/shard_map/while
  752.4 15.8 %copy-start.41 = (f32[3,3,512]{2,1,0:T(4,128)}, f32[3,3,512]{2,1,0:T(4,128)S(1)}, u32[]{:S(2)}) copy-start(f32[3,3,512]{2,1,0:T(4,128)S(1)} %get-tuple-element.470) | copy-start | bytes 55300 | tf_op jit(solution)/shard_map/while
  781.0 30.7 %copy-start.16 = (f32[1024,576]{0,1:T(8,128)}, f32[1024,576]{0,1:T(8,128)S(1)}, u32[]{:S(2)}) copy-start(f32[1024,576]{0,1:T(8,128)S(1)} %get-tuple-element.475) | copy-start | bytes 7077892 | tf_op jit(solution)/shard_map/while
  926.0 15.2 copy-start.48
  926.0 15.3 copy-start.18
  953.8 245.3 %reduce-scatter.3.cloned.1.call-start = ((), (), s32[]{:S(2)}) async-start(), calls=%async_computation.2 | async-start | bytes 15925248 | tf_op jit(solution)/shard_map/reduce_scatter | solution.py:318
  954.4 292.0 %copy-start.45 = (f32[72,6144]{1,0:T(8,128)S(1)}, f32[72,6144]{1,0:T(8,128)}, u32[]{:S(2)}) copy-start(f32[72,6144]{1,0:T(8,128)} %param.31) | copy-start | bytes 5308420
  954.4 292.0 %all-reduce.5.cloned.1.call-start = ((), (), s32[]{:S(2)}) async-start(), calls=%async_computation.3 | async-start | bytes 3538944 | tf_op jit(solution)/shard_map/psum | solution.py:321
  1199.2 116.2 %all-gather.9.cloned.1.call-start = ((), (), s32[]{:S(2)}) async-start(), calls=%async_computation.4 | async-start | bytes 3981312 | tf_op jit(solution)/shard_map/all_gather | solution.py:331
  1250.8 306.9 %all-gather.11.cloned.1.call-start = ((), (), s32[]{:S(2)}) async-start(), calls=%async_computation.5 | async-start | bytes 2211840 | tf_op jit(solution)/shard_map/all_gather | solution.py:340
  1315.4 199.5 %copy-start.50 = (f32[576,2]{0,1:T(2,128)S(1)}, f32[576,2]{0,1:T(2,128)}, u32[]{:S(2)}) copy-start(f32[576,2]{0,1:T(2,128)} %get-tuple-element.254) | copy-start | bytes 13828
  1315.4 224.7 %copy-start.53 = (f32[2,72]{1,0:T(2,128)S(1)}, f32[2,72]{1,0:T(2,128)}, u32[]{:S(2)}) copy-start(f32[2,72]{1,0:T(2,128)} %param.30) | copy-start | bytes 1732
  1315.4 241.7 %copy-start.52 = (f32[2,72]{1,0:T(2,128)S(1)}, f32[2,72]{1,0:T(2,128)}, u32[]{:S(2)}) copy-start(f32[2,72]{1,0:T(2,128)} %param.28) | copy-start | bytes 1732
  1540.7 20.5 %copy-start.51 = (f32[2,72]{1,0:T(2,128)}, f32[2,72]{1,0:T(2,128)S(1)}, u32[]{:S(2)}) copy-start(f32[2,72]{1,0:T(2,128)S(1)} %get-tuple-element.318) | copy-start | bytes 1732
  (88 other events, 420.1 us)
Sparse Core Ops, SparseCore 0:
  29.3 228.8 all-gather.12
  499.0 225.8 all-gather.12
Sparse Core Ops, SparseCore 1:
  957.9 241.1 reduce-scatter.2
  1201.4 44.9 all-reduce.4
  1250.9 64.4 all-gather.8
  1513.1 18.4 all-gather.10
